TPU v7x, 128 devices: a whole 4x4x4 slice. The times are simulated.
128 devices in a mesh: filt: 8 (over z, x_hi), space: 16 (over x_lo, y, core).
Axes of the slice: x: 4 (x_hi: 2, x_lo: 2; x = x_hi * 2 + x_lo), y: 4, z: 4, core: 2. Of those that a mesh axis runs over, the one named last changes fastest.
Arguments:
- inputs: bfloat16 [16, 256, 2048], P('space', 'filt'), may hold values from -6 to 6
- weight: bfloat16 [3, 3, 3, 256, 256], P(None, None, None, 'filt'), may hold values from -0.078125 to 0.078125
- bias: bfloat16 [256], P('filt'), may hold values from -4 to 4
- cotangent: bfloat16 [16, 256, 2048], P('space', 'filt'), may hold values from -6 to 6
Outputs:
- output: float32 [16, 256, 2048], P('space', 'filt')
- grad_inputs: float32 [16, 256, 2048], P('space', 'filt')
- grad_weight: float32 [3, 3, 3, 256, 256], P(None, None, None, 'filt')
- grad_bias: float32 [256], P('filt')
All inputs are finite; a program needn't handle non-finite values.
Results may differ from a plain program's by a relative error of at most 0.0003.
Values may be sent and summed in bfloat16 or wider, within the bound.
No kernel may reach another device: no remote copies, remote signals or barrier semaphores. Data moves between devices by JAX's collectives and lax.ppermute only.
A program may use at most 64 MiB of HBM per device.

v0:
```python
import jax
import jax.numpy as jnp
from jax import lax
from jax.sharding import PartitionSpec as P

ROWS = 32
WIDE = 64


def extended(cells, sides, width):
    for axis, dim in sides:
        count = lax.axis_size(axis)
        ends = count - 1
        head = lax.slice_in_dim(cells, 0, width, axis=dim)
        tail = lax.slice_in_dim(cells, cells.shape[dim] - width, cells.shape[dim], axis=dim)
        cells = jnp.concatenate(
            [
                lax.ppermute(tail, axis, [(i, (i + 1) % count) for i in range(ends)]),
                cells,
                lax.ppermute(head, axis, [((i + 1) % count, i) for i in range(ends)]),
            ],
            axis=dim,
        )
    return cells


def convolve_padded(padded, kernel):
    volume = padded.reshape(padded.shape[0], padded.shape[1], ROWS, WIDE)
    result = lax.conv_general_dilated(
        volume[None],
        kernel,
        (1, 1, 1),
        [(0, 0), (1, 1), (1, 1)],
        dimension_numbers=("NDCHW", "DHWIO", "NDCHW"),
        preferred_element_type=jnp.float32,
    )
    return result[0].reshape(result.shape[1], result.shape[2], ROWS * WIDE)


def body(inputs, weight, bias, cotangent):
    planes = inputs.shape[0]
    own_channels = inputs.shape[1]
    padded_in = extended(inputs, (("space", 0),), 1)
    partial_out = convolve_padded(padded_in, weight)
    summed = lax.psum_scatter(partial_out, "filt", scatter_dimension=1, tiled=True)
    output = summed + bias.astype(jnp.float32)[None, :, None]
    all_grad = lax.all_gather(cotangent, "filt", axis=1, tiled=True)
    padded_grad = extended(all_grad, (("space", 0),), 1)
    back_kernel = jnp.swapaxes(jnp.flip(weight, (0, 1, 2)), 3, 4)
    grad_inputs = convolve_padded(padded_grad, back_kernel)
    shaped_in = padded_in.reshape(planes + 2, own_channels, ROWS, WIDE)
    framed = jnp.pad(shaped_in, ((0, 0), (0, 0), (1, 1), (1, 1)))
    grad_vol = all_grad.reshape(planes, all_grad.shape[1], ROWS, WIDE)
    terms = []
    for depth_off in range(3):
        for row_off in range(3):
            for col_off in range(3):
                window = framed[
                    depth_off : depth_off + planes,
                    :,
                    row_off : row_off + ROWS,
                    col_off : col_off + WIDE,
                ]
                terms.append(
                    lax.dot_general(
                        window,
                        grad_vol,
                        (((0, 2, 3), (0, 2, 3)), ((), ())),
                        preferred_element_type=jnp.float32,
                    )
                )
    kernel_part = jnp.stack(terms).reshape(3, 3, 3, own_channels, grad_vol.shape[1])
    bias_part = jnp.sum(cotangent.astype(jnp.float32), axis=(0, 2))
    kernel_total, bias_total = lax.psum((kernel_part, bias_part), "space")
    factor = 1.0 / jnp.sqrt(jnp.float32(planes * lax.axis_size("space") * ROWS * WIDE))
    return (output, grad_inputs, kernel_total * factor, bias_total * factor)


def solution(mesh):
    placed = (
        P("space", "filt", None),
        P(None, None, None, "filt", None),
        P("filt"),
        P("space", "filt", None),
    )
    return jax.shard_map(
        body,
        mesh=mesh,
        in_specs=placed,
        out_specs=(
            P("space", "filt", None),
            P("space", "filt", None),
            P(None, None, None, "filt", None),
            P("filt"),
        ),
        check_vma=False,
    )
```

profile of v0, /device:TPU:1, one launch (start us, length us, event | category | flops | bytes accessed | tf_op | source)
XLA Modules:
  0.0 326.3 jit_solution(3926293909356311096)
XLA Ops:
  7.2 4.7 %collective-permute-start = (bf16[1,32,2048]{2,1,0:T(8,128)(2,1)}, bf16[1,32,2048]{2,1,0:T(8,128)(2,1)S(1)}, u32[]{:S(2)}, u32[]{:S(2)}) collective-permute-start(bf16[1,32,2048]{2,1,0:T(8,128)(2,1)} %param.4), channel_id=1, source_target_pairs={{0,1},{1,2},{2,3},{3,4},{4,5},{5,6},{6,7},{7,8},{8,9},{9,10},{10,1... | collective-permute-start | bytes 393224 | tf_op jit(solution)/shard_map/ppermute | solution.py:18
  12.0 1.9 collective-permute-start.1
  14.0 0.2 collective-permute-done
  14.2 1.0 constant_dynamic-update-slice_fusion.1
  15.2 3.4 %collective-permute-done.1 = bf16[1,32,2048]{2,1,0:T(8,128)(2,1)S(1)} collective-permute-done((bf16[1,32,2048]{2,1,0:T(8,128)(2,1)}, bf16[1,32,2048]{2,1,0:T(8,128)(2,1)S(1)}, u32[]{:S(2)}, u32[]{:S(2)}) %collective-permute-start.1) | collective-permute-done | bytes 131104 | tf_op jit(solution)/shard_map/ppermute | solution.py:20
  18.5 0.8 reshape.169
  19.3 0.8 reshape.214
  20.2 0.3 copy.47
  20.5 2.1 copy.50
  22.6 3.0 pad.5.clone
  25.6 3.9 %copy.35 = bf16[3,32,32,1,8,9]{1,4,5,2,0,3:T(8,128)(2,1)} copy(bf16[3,32,32,1,8,9]{2,1,5,4,0,3:T(8,128)(2,1)} %bitcast.299) | data formatting | bytes 884736 | tf_op jit(solution)/shard_map/conv_general_dilated | solution.py:29
  29.5 1.1 slice.109
  30.7 3.9 %fusion.17 = f32[1,32,8,9,256]{4,2,3,1,0:T(8,128)S(1)} fusion(bf16[3,3,3,32,256]{4,3,2,1,0:T(8,128)(2,1)S(1)} %copy-done, bf16[3,32,32,1,7,2]{1,4,5,2,0,3:T(8,128)(2,1)S(1)} %slice.109, bf16[3,32,32,1,8,9]{1,4,5,2,0,3:T(8,128)(2,1)} %copy.35, pred[8,9]{0,1:T(8,128)(4,1)S(1)} %copy-done.9), kind=kOutput, calls=%fused_computation.19 | convolution fusion | flops 1000194048 | bytes 3330120 | tf_op jit(solution)/shard_map/conv_general_dilated | solution.py:29
  34.6 0.8 copy.36
  35.3 0.2 slice_bitcast_fusion
  35.6 2.5 copy.37
  38.1 6.1 %copy.38 = f32[1,256,2048]{2,0,1:T(1,128)} copy(f32[1,256,2048]{1,2,0:T(8,128)} %bitcast.298) | data formatting | bytes 4194304 | tf_op jit(solution)/shard_map/reshape;squeeze | solution.py:37
  44.5 14.0 %all-gather.2.cloned.1.call-done = bf16[1,256,2048]{2,1,0:T(8,128)(2,1)} async-done(((bf16[1,32,2048]{2,1,0:T(8,128)(2,1)}), bf16[1,256,2048]{2,1,0:T(8,128)(2,1)}) %all-gather.2.cloned.1.call-update) | async-done | bytes 1048592 | tf_op jit(solution)/shard_map/all_gather | solution.py:47
  58.5 1.5 copy.39
  60.0 0.4 fusion.49
  60.5 0.3 fusion.48
  60.8 0.4 fusion.47
  61.2 0.4 fusion.46
  61.7 0.4 fusion.45
  62.1 0.4 fusion.44
  62.5 0.4 fusion.43
  62.9 0.3 fusion.42
  63.3 0.4 fusion.41
  63.7 0.4 fusion.40
  64.1 0.3 fusion.39
  64.4 0.4 fusion.38
  64.9 0.4 fusion.37
  65.3 0.4 fusion.36
  65.7 0.4 fusion.35
  66.1 0.4 fusion.34
  66.5 0.3 fusion.33
  66.9 0.4 fusion.32
  67.3 0.4 fusion.31
  67.7 0.3 fusion.30
  68.0 0.4 fusion.29
  68.5 0.4 fusion.28
  68.9 0.4 fusion.27
  69.3 0.4 fusion.26
  69.7 0.4 fusion.25
  70.2 0.3 fusion.24
  70.5 0.4 fusion.23
  70.9 0.9 copy-done.2
  71.9 0.6 dynamic-slice
  73.1 4.2 %collective-permute-start.3 = (bf16[1,256,2048]{1,2,0:T(8,128)(2,1)S(1)}, bf16[1,256,2048]{1,2,0:T(8,128)(2,1)S(1)}, u32[]{:S(2)}, u32[]{:S(2)}) collective-permute-start(bf16[1,256,2048]{1,2,0:T(8,128)(2,1)S(1)} %copy.39), channel_id=1, source_target_pairs={{1,0},{2,1},{3,2},{4,3},{5,4},{6,5},{7,6},{8,7},{9,8},{10,9},{11,1... | collective-permute-start | bytes 3145736 | tf_op jit(solution)/shard_map/ppermute | solution.py:20
  77.3 3.0 collective-permute-start.2
  80.5 45.1 %psum.15 = f32[32]{0:T(128)S(1)} all-reduce(f32[32]{0:T(128)S(1)} %convert_reduce_fusion), channel_id=1, replica_groups=mesh['filt'=8,'space'=16] {'space'}, use_global_device_ids=true, to_apply=%region_3.4 | all-reduce | flops 32 | bytes 256 | tf_op jit(solution)/shard_map/psum | solution.py:74
  125.6 0.5 broadcast_multiply_fusion.1
  126.1 52.8 %all-reduce.7.cloned.1.call-done = f32[1,256,2048]{2,0,1:T(1,128)} async-done(((f32[1,256,2048]{2,0,1:T(1,128)}), f32[1,256,2048]{2,0,1:T(1,128)}) %all-reduce.7.cloned.1.call-update) | async-done | bytes 2097168
  178.9 1.2 dynamic-slice_add_fusion
  180.1 0.8 copy.49
  180.8 119.8 %all-reduce.5.cloned.1.call-done = f32[3,3,3,32,256]{4,3,2,1,0:T(8,128)} async-done(((f32[3,3,3,32,256]{4,3,2,1,0:T(8,128)}), f32[3,3,3,32,256]{4,3,2,1,0:T(8,128)}) %all-reduce.5.cloned.1.call-update) | async-done | bytes 884752 | tf_op jit(solution)/shard_map/psum | solution.py:74
  300.6 2.2 broadcast_multiply_fusion
  302.8 1.6 pad_maximum_fusion
  304.4 1.8 copy.51
  306.2 0.4 pad.7.clone
  306.6 2.1 copy.44
  308.9 8.9 %fusion.20 = f32[1,32,8,9,32]{4,2,3,1,0:T(8,128)S(1)} fusion(bf16[3,3,3,32,256]{4,3,2,1,0:T(8,128)(2,1)S(1)} %copy-done, bf16[3,256,32,1,7,2]{1,4,5,2,0,3:T(8,128)(2,1)S(1)} %slice.111, bf16[3,256,32,1,8,9]{1,4,5,2,0,3:T(8,128)(2,1)S(1)} %copy.44, pred[8,9]{0,1:T(8,128)(4,1)S(1)} %copy-done.10), kind=kOutput, calls=%fused_computation.20 | convolution fusion | flops 1011032064 | bytes 4964424 | tf_op jit(solution)/shard_map/conv_general_dilated | solution.py:29
  318.1 0.8 copy.46
  318.8 0.9 reshape_squeeze.7
  (36 shorter events, 1.1 us)
Async XLA Ops:
  7.2 23.5 %copy-start = (bf16[3,3,3,32,256]{4,3,2,1,0:T(8,128)(2,1)S(1)}, bf16[3,3,3,32,256]{4,3,2,1,0:T(8,128)(2,1)}, u32[]{:S(2)}) copy-start(bf16[3,3,3,32,256]{4,3,2,1,0:T(8,128)(2,1)} %param.5) | copy-start | bytes 1327108
  7.2 51.4 %all-gather.2.cloned.1.call-start = ((), (), s32[]{:S(2)}) async-start(), calls=%async_computation | async-start | bytes 1179648 | tf_op jit(solution)/shard_map/all_gather | solution.py:47
  7.2 7.0 %collective-permute-start = (bf16[1,32,2048]{2,1,0:T(8,128)(2,1)}, bf16[1,32,2048]{2,1,0:T(8,128)(2,1)S(1)}, u32[]{:S(2)}, u32[]{:S(2)}) collective-permute-start(bf16[1,32,2048]{2,1,0:T(8,128)(2,1)} %param.4), channel_id=1, source_target_pairs={{0,1},{1,2},{2,3},{3,4},{4,5},{5,6},{6,7},{7,8},{8,9},{9,10},{10,1... | collective-permute-start | bytes 393224 | tf_op jit(solution)/shard_map/ppermute | solution.py:18
  12.0 166.9 %all-reduce.7.cloned.1.call-start = ((), (), s32[]{:S(2)}) async-start(), calls=%async_computation.2 | async-start | bytes 4194304
  12.0 6.5 %collective-permute-start.1 = (bf16[1,32,2048]{2,1,0:T(8,128)(2,1)}, bf16[1,32,2048]{2,1,0:T(8,128)(2,1)S(1)}, u32[]{:S(2)}, u32[]{:S(2)}) collective-permute-start(bf16[1,32,2048]{2,1,0:T(8,128)(2,1)} %param.4), channel_id=1, source_target_pairs={{1,0},{2,1},{3,2},{4,3},{5,4},{6,5},{7,6},{8,7},{9,8},{10,9},{11,1... | collective-permute-start | bytes 393224 | tf_op jit(solution)/shard_map/ppermute | solution.py:20
  14.2 4.3 %copy-start.4 = (bf16[1,32,2048]{2,1,0:T(8,128)(2,1)}, bf16[1,32,2048]{2,1,0:T(8,128)(2,1)S(1)}, u32[]{:S(2)}) copy-start(bf16[1,32,2048]{2,1,0:T(8,128)(2,1)S(1)} %collective-permute-done) | copy-start | bytes 393220
  25.6 5.1 %copy-start.9 = (pred[8,9]{0,1:T(8,128)(4,1)S(1)}, pred[8,9]{0,1:T(8,128)(4,1)}, u32[]{:S(2)}) copy-start(pred[8,9]{0,1:T(8,128)(4,1)} %constant.20) | copy-start | bytes 220
  44.3 256.4 %all-reduce.5.cloned.1.call-start = ((), (), s32[]{:S(2)}) async-start(), calls=%async_computation.1 | async-start | bytes 1769472 | tf_op jit(solution)/shard_map/psum | solution.py:74
  60.4 1.2 copy-start.1
  60.5 1.2 copy-start.5
  64.1 1.2 copy-start.3
  70.1 1.7 copy-start.7
  70.2 1.7 copy-start.8
  70.2 10.2 %copy-start.6 = (bf16[1,32,2048]{2,1,0:T(8,128)(2,1)S(1)}, bf16[1,32,2048]{2,1,0:T(8,128)(2,1)}, u32[]{:S(2)}) copy-start(bf16[1,32,2048]{2,1,0:T(8,128)(2,1)} %param.7) | copy-start | bytes 393220
  70.9 0.9 copy-start.2
  73.1 229.7 %collective-permute-start.3 = (bf16[1,256,2048]{1,2,0:T(8,128)(2,1)S(1)}, bf16[1,256,2048]{1,2,0:T(8,128)(2,1)S(1)}, u32[]{:S(2)}, u32[]{:S(2)}) collective-permute-start(bf16[1,256,2048]{1,2,0:T(8,128)(2,1)S(1)} %copy.39), channel_id=1, source_target_pairs={{1,0},{2,1},{3,2},{4,3},{5,4},{6,5},{7,6},{8,7},{9,8},{10,9},{11,1... | collective-permute-start | bytes 3145736 | tf_op jit(solution)/shard_map/ppermute | solution.py:20
  77.3 225.5 %collective-permute-start.2 = (bf16[1,256,2048]{1,2,0:T(8,128)(2,1)S(1)}, bf16[1,256,2048]{1,2,0:T(8,128)(2,1)}, u32[]{:S(2)}, u32[]{:S(2)}) collective-permute-start(bf16[1,256,2048]{1,2,0:T(8,128)(2,1)S(1)} %copy.39), channel_id=1, source_target_pairs={{0,1},{1,2},{2,3},{3,4},{4,5},{5,6},{6,7},{7,8},{8,9},{9,10},{10,1... | collective-permute-start | bytes 3145736 | tf_op jit(solution)/shard_map/ppermute | solution.py:18
  306.6 2.3 copy-start.10
Sparse Core Ops, SparseCore 0:
  12.1 46.3 all-gather.1
  61.1 117.7 all-reduce.6
  181.9 118.6 all-reduce.4
where the time goes:
time: 327 us; the launch traced here: 326 us
  waiting for transfers between devices  190 us (58%)
  blocking collectives  45.1 us (14%)
  local copies, waits for them, and re-layouts  33 us (10%)
  matrix products  23.5 us (7%)
  between operations  14.8 us (5%)
  starting transfers between devices  14.1 us (4%)
  other arithmetic  5.6 us (2%)
    psum x1, waiting for transfers between devices, body(): kernel_total, bias_total = lax.psum((kernel_part, bias_part), 'space')  120 us
    unnamed x4, waiting for transfers between devices  52.8 us
    psum x1, blocking collectives, body(): kernel_total, bias_total = lax.psum((kernel_part, bias_part), 'space')  45.1 us
    all_gather x1, waiting for transfers between devices, body(): all_grad = lax.all_gather(cotangent, 'filt', axis=1, tiled=True)  14 us
    conv_general_dilated x2, matrix products, convolve_padded(): lax.conv_general_dilated(volume[None], kernel, (1, 1, 1), [(0, 0), (1, 1)...  12.8 us
    conv_general_dilated x10, local copies, waits for them, and re-layouts, convolve_padded(): lax.conv_general_dilated(volume[None], kernel, (1, 1, 1), [(0, 0), (1, 1)...  11.9 us
    dot_general x27, matrix products, body(): lax.dot_general(window, grad_vol, (((0, 2, 3), (0, 2, 3)), ((), ())), pre...  10.7 us
    ppermute x2, starting transfers between devices, extended(): lax.ppermute(tail, axis, [(i, (i + 1) % count) for i in range(ends)])  7.73 us
  transfers between devices with their start and end apart: 7, of which 5 were waited for; matrix products, arithmetic and copies ran while one was open for 14% of the time, Pallas kernels for 0%

commit v1 on v0

--- a/solution.py
+++ b/solution.py
@@ -44,7 +44,9 @@
     partial_out = convolve_padded(padded_in, weight)
     summed = lax.psum_scatter(partial_out, "filt", scatter_dimension=1, tiled=True)
     output = summed + bias.astype(jnp.float32)[None, :, None]
-    all_grad = lax.all_gather(cotangent, "filt", axis=1, tiled=True)
+    all_grad = jnp.concatenate(
+        lax.all_to_all(jnp.stack([cotangent] * lax.axis_size("filt")), "filt", 0, 0), axis=1
+    )
     padded_grad = extended(all_grad, (("space", 0),), 1)
     back_kernel = jnp.swapaxes(jnp.flip(weight, (0, 1, 2)), 3, 4)
     grad_inputs = convolve_padded(padded_grad, back_kernel)

time: 327 us -> 307 us (0.939)
  waiting for transfers between devices: 190 us -> 161 us
  local copies, waits for them, and re-layouts: 33 us -> 54.5 us
  blocking collectives: 45.1 us -> 26.3 us
  starting transfers between devices: 14.1 us -> 20.1 us
    psum x1, waiting for transfers between devices: 120 us -> 70.9 us  [body(): kernel_total, bias_total = lax.psum((kernel_part, bias_part), 'space')]
    unnamed x4 -> x3, waiting for transfers between devices: 52.8 us -> 86.8 us
    psum x1, blocking collectives: 45.1 us -> 26.3 us  [body(): kernel_total, bias_total = lax.psum((kernel_part, bias_part), 'space')]
    all_gather x1 -> x0, waiting for transfers between devices: 14 us -> none  [body(): all_grad = lax.all_gather(cotangent, 'filt', axis=1, tiled=True)]
    another operation x0 -> x6, local copies, waits for them, and re-layouts: none -> 10.9 us
    all_to_all x0 -> x1, starting transfers between devices: none -> 8.31 us  [body(): lax.all_to_all(jnp.stack([cotangent] * lax.axis_size('filt')), 'filt', 0, 0)]
    concatenate x1 -> x4, local copies, waits for them, and re-layouts: 0.01 us -> 6.31 us  [extended(): jnp.concatenate([lax.ppermute(tail, axis, [(i, (i + 1) % count) for i in...]
    ppermute x0 -> x2, local copies, waits for them, and re-layouts: none -> 4.6 us  [the longest x1 2.34 us: extended(): lax.ppermute(tail, axis, [(i, (i + 1) % count) for i in range(ends)])]
  transfers between devices with their start and end apart: 7 -> 7, of which waited for: 5 -> 3; matrix products, arithmetic and copies ran while one was open for 14% -> 20% of each run, Pallas kernels for 0% -> 0%
where the time goes in v1:
time: 307 us; the launch traced here: 306 us
  waiting for transfers between devices  161 us (52%)
  local copies, waits for them, and re-layouts  54.5 us (18%)
  blocking collectives  26.3 us (9%)
  matrix products  23.4 us (8%)
  starting transfers between devices  20.1 us (7%)
  between operations  15 us (5%)
  other arithmetic  5.6 us (2%)
    unnamed x3, waiting for transfers between devices  86.8 us
    psum x1, waiting for transfers between devices, body(): kernel_total, bias_total = lax.psum((kernel_part, bias_part), 'space')  70.9 us
    psum x1, blocking collectives, body(): kernel_total, bias_total = lax.psum((kernel_part, bias_part), 'space')  26.3 us
    conv_general_dilated x2, matrix products, convolve_padded(): lax.conv_general_dilated(volume[None], kernel, (1, 1, 1), [(0, 0), (1, 1)...  12.9 us
    conv_general_dilated x10, local copies, waits for them, and re-layouts, convolve_padded(): lax.conv_general_dilated(volume[None], kernel, (1, 1, 1), [(0, 0), (1, 1)...  12.6 us
    dot_general x27, matrix products, body(): lax.dot_general(window, grad_vol, (((0, 2, 3), (0, 2, 3)), ((), ())), pre...  10.5 us
    another operation x5, local copies, waits for them, and re-layouts  8.81 us
    all_to_all x1, starting transfers between devices, body(): lax.all_to_all(jnp.stack([cotangent] * lax.axis_size('filt')), 'filt', 0, 0)  8.31 us
  transfers between devices with their start and end apart: 7, of which 3 were waited for; matrix products, arithmetic and copies ran while one was open for 20% of the time, Pallas kernels for 0%

profile of v1, /device:TPU:1, one launch (start us, length us, event | category | flops | bytes accessed | tf_op | source)
XLA Modules:
  0.0 306.2 jit_solution(5146965281777670745)
XLA Ops:
  7.2 2.1 stack.95
  9.3 8.3 %all-to-all-start = ((bf16[8,1,32,2048]{3,2,1,0:T(8,128)(2,1)}), bf16[8,1,32,2048]{3,2,1,0:T(8,128)(2,1)S(1)}, u32[]{:S(2)}, u32[]{:S(2)}) async-start(bf16[8,1,32,2048]{3,2,1,0:T(8,128)(2,1)} %stack.95), calls=%async_computation | async-start | bytes 2097152 | tf_op jit(solution)/shard_map/all_to_all | solution.py:48
  17.6 4.0 %collective-permute-start = (bf16[1,32,2048]{2,1,0:T(8,128)(2,1)S(1)}, bf16[1,32,2048]{2,1,0:T(8,128)(2,1)S(1)}, u32[]{:S(2)}, u32[]{:S(2)}) collective-permute-start(bf16[1,32,2048]{2,1,0:T(8,128)(2,1)S(1)} %copy-done.6), channel_id=1, source_target_pairs={{0,1},{1,2},{2,3},{3,4},{4,5},{5,6},{6,7},{7,8},{8,9},{9,10},{10,1... | collective-permute-start | bytes 393224 | tf_op jit(solution)/shard_map/ppermute | solution.py:18
  21.7 1.9 collective-permute-start.1
  23.6 1.0 reshape.186
  24.6 3.7 %collective-permute-done.1 = bf16[1,32,2048]{2,1,0:T(8,128)(2,1)S(1)} collective-permute-done((bf16[1,32,2048]{2,1,0:T(8,128)(2,1)S(1)}, bf16[1,32,2048]{2,1,0:T(8,128)(2,1)S(1)}, u32[]{:S(2)}, u32[]{:S(2)}) %collective-permute-start.1) | collective-permute-done | bytes 131104 | tf_op jit(solution)/shard_map/ppermute | solution.py:20
  28.3 0.8 reshape.171
  29.1 1.7 reshape.215
  31.1 3.1 %copy.141 = bf16[3,32,32,1,64]{2,1,4,0,3:T(8,128)(2,1)} copy(bf16[3,32,32,1,64]{4,2,1,0,3:T(8,128)(2,1)} %reshape.215) | data formatting | bytes 786432
  34.2 3.0 pad.5.clone
  37.1 3.9 %copy.97 = bf16[3,32,32,1,8,9]{1,4,5,2,0,3:T(8,128)(2,1)} copy(bf16[3,32,32,1,8,9]{2,1,5,4,0,3:T(8,128)(2,1)} %bitcast.274) | data formatting | bytes 884736 | tf_op jit(solution)/shard_map/conv_general_dilated | solution.py:29
  41.1 1.9 slice.109
  42.9 1.0 reshape.177
  43.9 1.0 reshape.195
  44.8 3.2 %reshape.173 = bf16[256,32,64]{2,1,0:T(8,128)(2,1)} reshape(bf16[8,1,32,2048]{3,2,1,0:T(8,128)(2,1)S(1)} %all-to-all-done) | data formatting | bytes 2097152 | tf_op jit(solution)/shard_map/reshape.6
  48.0 2.8 copy.110
  50.8 0.4 fusion.49
  51.6 0.4 fusion.47
  52.0 0.4 fusion.46
  52.4 0.4 fusion.45
  52.7 0.4 fusion.44
  53.2 0.4 fusion.43
  53.9 0.4 fusion.41
  54.3 0.4 fusion.40
  54.7 0.3 fusion.39
  55.1 0.4 fusion.38
  55.5 0.4 fusion.37
  55.9 0.4 fusion.36
  56.3 0.4 fusion.35
  56.7 0.4 fusion.34
  57.4 0.4 fusion.32
  57.9 0.4 fusion.31
  58.6 0.4 fusion.29
  59.0 0.4 fusion.28
  59.4 0.4 fusion.27
  59.8 0.4 fusion.26
  60.2 0.4 fusion.25
  61.0 0.4 fusion.23
  61.4 0.9 copy-done.5
  62.6 4.0 %fusion.17 = f32[1,32,8,9,256]{4,2,3,1,0:T(8,128)S(1)} fusion(bf16[3,3,3,32,256]{4,3,2,1,0:T(8,128)(2,1)S(1)} %copy-done, bf16[3,32,32,1,7,2]{1,4,5,2,0,3:T(8,128)(2,1)} %slice.109, bf16[3,32,32,1,8,9]{1,4,5,2,0,3:T(8,128)(2,1)} %copy.97, pred[8,9]{0,1:T(8,128)(4,1)S(1)} %copy-done.10), kind=kOutput, calls=%fused_computation.19 | convolution fusion | flops 1000194048 | bytes 3330120 | tf_op jit(solution)/shard_map/conv_general_dilated | solution.py:29
  66.6 0.8 copy.98
  67.4 1.9 collective-permute-start.3
  69.3 3.6 %collective-permute-start.2 = (bf16[1,256,2048]{2,1,0:T(8,128)(2,1)S(1)}, bf16[1,256,2048]{2,1,0:T(8,128)(2,1)}, u32[]{:S(2)}, u32[]{:S(2)}) collective-permute-start(bf16[1,256,2048]{2,1,0:T(8,128)(2,1)S(1)} %bitcast.271), channel_id=1, source_target_pairs={{0,1},{1,2},{2,3},{3,4},{4,5},{5,6},{6,7},{7,8},{8,9},{9,10},{10,1... | collective-permute-start | bytes 3145736 | tf_op jit(solution)/shard_map/ppermute | solution.py:18
  73.2 2.5 copy.99
  75.7 6.2 %copy.100 = f32[1,256,2048]{2,0,1:T(1,128)} copy(f32[1,256,2048]{1,2,0:T(8,128)} %bitcast.273) | data formatting | bytes 4194304 | tf_op jit(solution)/shard_map/reshape;squeeze | solution.py:37
  82.0 0.6 dynamic-slice
  83.4 26.3 %psum.15 = f32[32]{0:T(128)S(1)} all-reduce(f32[32]{0:T(128)S(1)} %convert_reduce_fusion), channel_id=1, replica_groups=mesh['filt'=8,'space'=16] {'space'}, use_global_device_ids=true, to_apply=%region_3.4 | all-reduce | flops 32 | bytes 256 | tf_op jit(solution)/shard_map/psum | solution.py:76
  109.6 0.5 broadcast_multiply_fusion.1
  110.1 3.2 %concatenate.15 = bf16[1,1,256,32,64]{4,3,2,1,0:T(8,128)(2,1)} reshape(bf16[8,1,32,2048]{3,2,1,0:T(8,128)(2,1)S(1)} %all-to-all-done) | data formatting | bytes 2097152 | tf_op jit(solution)/shard_map/concatenate | solution.py:16
  113.3 2.8 copy.103
  116.1 70.9 %all-reduce.5.cloned.1.call-done = f32[3,3,3,32,256]{4,3,2,1,0:T(8,128)} async-done(((f32[3,3,3,32,256]{4,3,2,1,0:T(8,128)}), f32[3,3,3,32,256]{4,3,2,1,0:T(8,128)}) %all-reduce.5.cloned.1.call-update) | async-done | bytes 884752 | tf_op jit(solution)/shard_map/psum | solution.py:76
  187.0 2.2 broadcast_multiply_fusion
  189.2 2.3 copy.102
  191.5 2.3 copy.101
  193.8 1.6 maximum_bitcast_fusion
  195.4 1.8 copy.142
  197.2 0.4 pad.7.clone
  197.5 2.1 copy.106
  199.8 8.9 %fusion.20 = f32[1,32,8,9,32]{4,2,3,1,0:T(8,128)S(1)} fusion(bf16[3,3,3,32,256]{4,3,2,1,0:T(8,128)(2,1)S(1)} %copy-done, bf16[3,256,32,1,7,2]{1,4,5,2,0,3:T(8,128)(2,1)S(1)} %slice.111, bf16[3,256,32,1,8,9]{1,4,5,2,0,3:T(8,128)(2,1)S(1)} %copy.106, pred[8,9]{0,1:T(8,128)(4,1)S(1)} %copy-done.10), kind=kOutput, calls=%fused_computation.20 | convolution fusion | flops 1011032064 | bytes 4964424 | tf_op jit(solution)/shard_map/conv_general_dilated | solution.py:29
  209.0 0.8 copy.108
  209.8 0.9 reshape_squeeze.7
  210.7 86.7 %all-reduce.7.cloned.1.call-done = f32[1,256,2048]{2,0,1:T(1,128)} async-done(((f32[1,256,2048]{2,0,1:T(1,128)}), f32[1,256,2048]{2,0,1:T(1,128)}) %all-reduce.7.cloned.1.call-update) | async-done | bytes 2097168
  297.4 1.2 dynamic-slice_add_fusion
  298.6 0.8 copy.140
  (44 shorter events, 3.2 us)
Async XLA Ops:
  7.2 55.4 %copy-start = (bf16[3,3,3,32,256]{4,3,2,1,0:T(8,128)(2,1)S(1)}, bf16[3,3,3,32,256]{4,3,2,1,0:T(8,128)(2,1)}, u32[]{:S(2)}) copy-start(bf16[3,3,3,32,256]{4,3,2,1,0:T(8,128)(2,1)} %param.5) | copy-start | bytes 1327108
  7.2 10.4 %copy-start.6 = (bf16[1,32,2048]{2,1,0:T(8,128)(2,1)S(1)}, bf16[1,32,2048]{2,1,0:T(8,128)(2,1)}, u32[]{:S(2)}) copy-start(bf16[1,32,2048]{2,1,0:T(8,128)(2,1)} %param.4) | copy-start | bytes 393220
  9.3 35.6 %all-to-all-start = ((bf16[8,1,32,2048]{3,2,1,0:T(8,128)(2,1)}), bf16[8,1,32,2048]{3,2,1,0:T(8,128)(2,1)S(1)}, u32[]{:S(2)}, u32[]{:S(2)}) async-start(bf16[8,1,32,2048]{3,2,1,0:T(8,128)(2,1)} %stack.95), calls=%async_computation | async-start | bytes 2097152 | tf_op jit(solution)/shard_map/all_to_all | solution.py:48
  17.6 169.4 %all-reduce.5.cloned.1.call-start = ((), (), s32[]{:S(2)}) async-start(), calls=%async_computation.1 | async-start | bytes 1769472 | tf_op jit(solution)/shard_map/psum | solution.py:76
  17.6 6.9 %collective-permute-start = (bf16[1,32,2048]{2,1,0:T(8,128)(2,1)S(1)}, bf16[1,32,2048]{2,1,0:T(8,128)(2,1)S(1)}, u32[]{:S(2)}, u32[]{:S(2)}) collective-permute-start(bf16[1,32,2048]{2,1,0:T(8,128)(2,1)S(1)} %copy-done.6), channel_id=1, source_target_pairs={{0,1},{1,2},{2,3},{3,4},{4,5},{5,6},{6,7},{7,8},{8,9},{9,10},{10,1... | collective-permute-start | bytes 393224 | tf_op jit(solution)/shard_map/ppermute | solution.py:18
  21.7 6.6 %collective-permute-start.1 = (bf16[1,32,2048]{2,1,0:T(8,128)(2,1)S(1)}, bf16[1,32,2048]{2,1,0:T(8,128)(2,1)S(1)}, u32[]{:S(2)}, u32[]{:S(2)}) collective-permute-start(bf16[1,32,2048]{2,1,0:T(8,128)(2,1)S(1)} %copy-done.6), channel_id=1, source_target_pairs={{1,0},{2,1},{3,2},{4,3},{5,4},{6,5},{7,6},{8,7},{9,8},{10,9},{11,1... | collective-permute-start | bytes 393224 | tf_op jit(solution)/shard_map/ppermute | solution.py:20
  51.2 1.2 copy-start.4
  54.7 1.2 copy-start.2
  58.3 1.2 copy-start.3
  60.6 1.9 copy-start.10
  61.4 0.9 copy-start.5
  62.3 235.1 %all-reduce.7.cloned.1.call-start = ((), (), s32[]{:S(2)}) async-start(), calls=%async_computation.2 | async-start | bytes 4194304
  67.4 121.8 %collective-permute-start.3 = (bf16[1,256,2048]{2,1,0:T(8,128)(2,1)S(1)}, bf16[1,256,2048]{2,1,0:T(8,128)(2,1)}, u32[]{:S(2)}, u32[]{:S(2)}) collective-permute-start(bf16[1,256,2048]{2,1,0:T(8,128)(2,1)S(1)} %bitcast.270), channel_id=1, source_target_pairs={{1,0},{2,1},{3,2},{4,3},{5,4},{6,5},{7,6},{8,7},{9,8},{10,9},{11,1... | collective-permute-start | bytes 3145736 | tf_op jit(solution)/shard_map/ppermute | solution.py:20
  69.3 122.2 %collective-permute-start.2 = (bf16[1,256,2048]{2,1,0:T(8,128)(2,1)S(1)}, bf16[1,256,2048]{2,1,0:T(8,128)(2,1)}, u32[]{:S(2)}, u32[]{:S(2)}) collective-permute-start(bf16[1,256,2048]{2,1,0:T(8,128)(2,1)S(1)} %bitcast.271), channel_id=1, source_target_pairs={{0,1},{1,2},{2,3},{3,4},{4,5},{5,6},{6,7},{7,8},{8,9},{9,10},{10,1... | collective-permute-start | bytes 3145736 | tf_op jit(solution)/shard_map/ppermute | solution.py:18
  75.7 6.2 %copy-start.8 = (bf16[32]{0:T(256)(128)(2,1)S(1)}, bf16[32]{0:T(256)(128)(2,1)}, u32[]{:S(2)}) copy-start(bf16[32]{0:T(256)(128)(2,1)} %param.6) | copy-start | bytes 196
  75.7 6.2 %copy-start.9 = (u32[128]{0:T(128)S(1)}, u32[128]{0:T(128)}, u32[]{:S(2)}) copy-start(u32[128]{0:T(128)} %constant.24) | copy-start | bytes 1540
  75.7 7.5 %copy-start.7 = (bf16[1,32,2048]{2,1,0:T(8,128)(2,1)S(1)}, bf16[1,32,2048]{2,1,0:T(8,128)(2,1)}, u32[]{:S(2)}) copy-start(bf16[1,32,2048]{2,1,0:T(8,128)(2,1)} %param.7) | copy-start | bytes 393220
  191.5 2.3 copy-start.1
Sparse Core Ops, SparseCore 0:
  62.5 124.4 all-reduce.4
  189.5 107.8 all-reduce.6
